TPU v7x, 32 devices: a whole 2x2x4 slice. The times are simulated.
32 devices in a mesh: tm: 16 (over z, y, x), col: 2 (over core).
Axes of the slice: x: 2, y: 2, z: 4, core: 2. Of those that a mesh axis runs over, the one named last changes fastest.
Arguments:
- rhs: float32 [16, 1024, 256], P('tm', 'col'), may hold values from -6 to 6
- inverse_blocks: float32 [3, 16, 1024, 1024], P(None, 'tm', None, 'col'), may hold values from -2 to 3, as said below
- lower_coupling: float32 [3, 16, 1024, 1024], P(None, 'tm', None, 'col'), may hold values from -0.1875 to 0.1875
- upper_coupling: float32 [3, 16, 1024, 1024], P(None, 'tm', None, 'col'), may hold values from -0.1875 to 0.1875
- tile_pattern: int32 [3, 16, 2, 8, 8], P(None, 'tm', None, None, 'col'), may hold values from 0 to 1, as said below
- tip_coupling: float32 [3, 16, 64, 1024], P(None, 'tm', None, 'col'), may hold values from -0.046875 to 0.046875
- tip_rhs: float32 [64, 256], replicated, may hold values from -6 to 6
Outputs:
- reduced: float32 [16, 1024, 256], P('tm', 'col')
- tip_reduced: float32 [64, 256], replicated
Inputs may be any that keep to these rules, and one draw needn't show every extreme that they name: Every inverse_blocks[l, j] is symmetric. tile_pattern[l, j, k, r, c] is 1 exactly where |r - c| is at most a half-width w[l, j, k] of 1 to 4; both half-widths 1 and 4 occur.
All inputs are finite; a program needn't handle non-finite values.
Results may differ from a plain program's by a relative error of at most 0.0001.
Values sent between devices are 32-bit elements; how exact they have to be, the bound alone decides.
A program may use at most 64 MiB of HBM per device.

v0:
```python
import jax
import jax.numpy as jnp
from jax import lax
from jax.sharding import PartitionSpec as P


def passed_along(block, axis, distance):
    devices = range(lax.axis_size(axis))
    route = [((i - distance) % len(devices), i) for i in devices]
    return lax.ppermute(block, axis, route)


def local(rhs, inverse_blocks, lower_coupling, upper_coupling, tile_pattern, tip_coupling, tip_rhs):
    highest = lax.Precision.HIGHEST
    own_cols = inverse_blocks.shape[3]
    block_order = inverse_blocks.shape[2]
    tiles_here = tile_pattern.shape[4]
    tiles_all = tile_pattern.shape[3]
    tile_size = block_order // tiles_all
    level_count = inverse_blocks.shape[0]

    def apply_pattern(coupling, pattern):
        reshaped_rows = coupling.reshape(tiles_all, tile_size, tiles_here, tile_size)
        masked = reshaped_rows * pattern.astype(jnp.float32)[:, None, :, None]
        return masked.reshape(block_order, own_cols)

    present_rows = rhs[0]
    pending = jnp.zeros(tip_rhs.shape, jnp.float32)
    for level_number in range(level_count):
        stride = 2**level_number
        lower_masked = apply_pattern(
            lower_coupling[level_number, 0], tile_pattern[level_number, 0, 0]
        )
        upper_masked = apply_pattern(
            upper_coupling[level_number, 0], tile_pattern[level_number, 0, 1]
        )
        inverse = inverse_blocks[level_number, 0]

        def row_term(first_row, row_count, input_rows=present_rows, inverse_here=inverse):
            return jnp.dot(
                inverse_here, input_rows, precision=highest, preferred_element_type=jnp.float32
            )

        solved = lax.psum_scatter(
            row_term(jnp.int32(0), own_cols * lax.axis_size("col")),
            "col",
            scatter_dimension=0,
            tiled=True,
        )
        whole_solved = lax.all_gather(solved, "col", axis=0, tiled=True)
        down_term = jnp.dot(
            lower_masked.T, whole_solved, precision=highest, preferred_element_type=jnp.float32
        )
        up_term = jnp.dot(
            upper_masked.T, whole_solved, precision=highest, preferred_element_type=jnp.float32
        )
        from_above = passed_along(down_term, "tm", -stride)
        from_below = passed_along(up_term, "tm", stride)
        present_rows = present_rows - from_above - from_below
        arrow_part = jnp.dot(
            tip_coupling[level_number, 0],
            solved,
            precision=highest,
            preferred_element_type=jnp.float32,
        )
        pending = pending + arrow_part
    tip_total = tip_rhs - lax.psum(pending, ("tm", "col"))
    return (present_rows[None], tip_total)


def solution(mesh):
    return jax.shard_map(
        local,
        mesh=mesh,
        in_specs=(
            P("tm", "col", None),
            P(None, "tm", None, "col"),
            P(None, "tm", None, "col"),
            P(None, "tm", None, "col"),
            P(None, "tm", None, None, "col"),
            P(None, "tm", None, "col"),
            P(),
        ),
        out_specs=(P("tm", "col", None), P()),
        check_vma=False,
    )
```

profile of v0, /device:TPU:1, one launch (start us, length us, event | category | flops | bytes accessed | tf_op | source)
XLA Modules:
  0.0 310.0 jit_solution(16763351207113429849)
XLA Ops:
  7.2 0.0 reduce-scatter.4.cloned.1.call-start
  7.2 4.5 %fusion.21 = f32[1024,256]{1,0:T(8,128)} fusion(f32[3,1,1024,512]{3,2,1,0:T(8,128)} %param.8, f32[1,512,256]{2,1,0:T(8,128)} %param.7), kind=kOutput, calls=%fused_computation.27 | convolution fusion | flops 1610612736 | bytes 3670016 | tf_op jit(solution)/shard_map/dot_general | solution.py:40
  11.7 0.0 reduce-scatter.4.cloned.1.call-update
  11.7 0.0 all-gather.4.cloned.1.call-start
  11.8 11.0 %reduce-scatter.4.cloned.1.call-done = f32[512,256]{1,0:T(8,128)} async-done(((f32[1024,256]{1,0:T(8,128)}), f32[512,256]{1,0:T(8,128)}) %reduce-scatter.4.cloned.1.call-update) | async-done | bytes 524304 | tf_op jit(solution)/shard_map/reduce_scatter | solution.py:44
  22.8 0.0 all-gather.4.cloned.1.call-update
  22.8 0.0 reduce-scatter.6.cloned.1.call-start
  22.9 0.1 copy.9
  23.0 0.1 copy.10
  23.0 11.5 %all-gather.4.cloned.1.call-done = f32[1024,256]{1,0:T(8,128)} async-done(((f32[512,256]{1,0:T(8,128)}), f32[1024,256]{1,0:T(8,128)}) %all-gather.4.cloned.1.call-update) | async-done | bytes 1048592 | tf_op jit(solution)/shard_map/all_gather | solution.py:50
  34.5 0.3 mul.66
  34.9 0.9 copy-done
  35.8 5.1 %fusion.10 = f32[512,256]{1,0:T(8,128)S(1)} fusion(f32[1024,256]{1,0:T(8,128)S(1)} %copy-done, f32[128,8,4,128]{3,2,1,0:T(4,128)S(1)} %bitcast.121, f32[3,1,1024,512]{3,2,1,0:T(8,128)} %param.9), kind=kOutput, calls=%fused_computation.16 | convolution fusion | flops 1611137024 | bytes 5767168 | tf_op jit(solution)/shard_map/dot_general | solution.py:51
  40.8 5.3 %collective-permute-start = (f32[512,256]{1,0:T(8,128)S(1)}, f32[512,256]{1,0:T(8,128)S(1)}, u32[]{:S(2)}, u32[]{:S(2)}) collective-permute-start(f32[512,256]{1,0:T(8,128)S(1)} %fusion.10), channel_id=1, source_target_pairs={{2,0},{4,2},{6,4},{8,6},{10,8},{12,10},{14,12},{16,14},{18,16},{20... | collective-permute-start | bytes 1572872 | tf_op jit(solution)/shard_map/ppermute | solution.py:10
  46.1 0.3 mul.69
  46.4 0.0 copy-start.3
  46.4 5.1 %fusion.8 = f32[512,256]{1,0:T(8,128)S(1)} fusion(f32[1024,256]{1,0:T(8,128)S(1)} %copy-done, f32[128,8,4,128]{3,2,1,0:T(4,128)S(1)} %bitcast.118, f32[3,1,1024,512]{3,2,1,0:T(8,128)} %param.10), kind=kOutput, calls=%fused_computation.13 | convolution fusion | flops 1611137024 | bytes 5767168 | tf_op jit(solution)/shard_map/dot_general | solution.py:54
  51.6 0.2 collective-permute-start.1
  51.8 5.3 %collective-permute-done = f32[512,256]{1,0:T(8,128)S(1)} collective-permute-done((f32[512,256]{1,0:T(8,128)S(1)}, f32[512,256]{1,0:T(8,128)S(1)}, u32[]{:S(2)}, u32[]{:S(2)}) %collective-permute-start) | collective-permute-done | bytes 524320 | tf_op jit(solution)/shard_map/ppermute | solution.py:10
  57.1 11.2 %collective-permute-done.1 = f32[512,256]{1,0:T(8,128)S(1)} collective-permute-done((f32[512,256]{1,0:T(8,128)S(1)}, f32[512,256]{1,0:T(8,128)S(1)}, u32[]{:S(2)}, u32[]{:S(2)}) %collective-permute-start.1) | collective-permute-done | bytes 524320 | tf_op jit(solution)/shard_map/ppermute | solution.py:10
  68.4 0.1 fusion.41
  68.5 6.1 %fusion.33 = f32[1024,256]{0,1:T(8,128)} fusion(f32[512,256]{1,0:T(8,128)S(1)} %fusion.41, f32[3,1,1024,512]{3,2,1,0:T(8,128)} %param.8), kind=kOutput, calls=%fused_computation.39 | convolution fusion | flops 1610612736 | bytes 3670016 | tf_op jit(solution)/shard_map/dot_general | solution.py:40
  74.6 0.0 reduce-scatter.6.cloned.1.call-update
  74.6 0.0 all-gather.6.cloned.1.call-start
  74.7 10.2 %reduce-scatter.6.cloned.1.call-done = f32[512,256]{0,1:T(8,128)} async-done(((f32[1024,256]{0,1:T(8,128)}), f32[512,256]{0,1:T(8,128)}) %reduce-scatter.6.cloned.1.call-update) | async-done | bytes 524304 | tf_op jit(solution)/shard_map/reduce_scatter | solution.py:44
  84.9 0.0 all-gather.6.cloned.1.call-update
  84.9 0.0 reduce-scatter.8.cloned.1.call-start
  84.9 0.1 copy.11
  85.0 0.1 copy.12
  85.1 11.4 %all-gather.6.cloned.1.call-done = f32[1024,256]{0,1:T(8,128)} async-done(((f32[512,256]{0,1:T(8,128)}), f32[1024,256]{0,1:T(8,128)}) %all-gather.6.cloned.1.call-update) | async-done | bytes 1048592 | tf_op jit(solution)/shard_map/all_gather | solution.py:50
  96.5 0.3 mul.72
  96.9 0.9 copy-done.2
  97.7 5.0 %fusion.6 = f32[512,256]{1,0:T(8,128)S(1)} fusion(f32[1024,256]{0,1:T(8,128)S(1)} %copy-done.2, f32[128,8,4,128]{3,2,1,0:T(4,128)S(1)} %bitcast.122, f32[3,1,1024,512]{3,2,1,0:T(8,128)} %param.9), kind=kOutput, calls=%fused_computation.10 | convolution fusion | flops 1611137024 | bytes 5767168 | tf_op jit(solution)/shard_map/dot_general | solution.py:51
  102.8 4.4 %collective-permute-start.2 = (f32[512,256]{1,0:T(8,128)S(1)}, f32[512,256]{1,0:T(8,128)S(1)}, u32[]{:S(2)}, u32[]{:S(2)}) collective-permute-start(f32[512,256]{1,0:T(8,128)S(1)} %fusion.6), channel_id=1, source_target_pairs={{4,0},{6,2},{8,4},{10,6},{12,8},{14,10},{16,12},{18,14},{20,16},{2... | collective-permute-start | bytes 1572872 | tf_op jit(solution)/shard_map/ppermute | solution.py:10
  107.2 0.3 mul.75
  107.5 5.0 %fusion.4 = f32[512,256]{1,0:T(8,128)S(1)} fusion(f32[1024,256]{0,1:T(8,128)S(1)} %copy-done.2, f32[128,8,4,128]{3,2,1,0:T(4,128)S(1)} %bitcast.119, f32[3,1,1024,512]{3,2,1,0:T(8,128)} %param.10), kind=kOutput, calls=%fused_computation.7 | convolution fusion | flops 1611137024 | bytes 5767168 | tf_op jit(solution)/shard_map/dot_general | solution.py:54
  112.5 0.3 collective-permute-start.3
  112.8 5.4 %collective-permute-done.2 = f32[512,256]{1,0:T(8,128)S(1)} collective-permute-done((f32[512,256]{1,0:T(8,128)S(1)}, f32[512,256]{1,0:T(8,128)S(1)}, u32[]{:S(2)}, u32[]{:S(2)}) %collective-permute-start.2) | collective-permute-done | bytes 524320 | tf_op jit(solution)/shard_map/ppermute | solution.py:10
  118.2 10.3 %collective-permute-done.3 = f32[512,256]{1,0:T(8,128)S(1)} collective-permute-done((f32[512,256]{1,0:T(8,128)S(1)}, f32[512,256]{1,0:T(8,128)S(1)}, u32[]{:S(2)}, u32[]{:S(2)}) %collective-permute-start.3) | collective-permute-done | bytes 524320 | tf_op jit(solution)/shard_map/ppermute | solution.py:10
  128.5 6.1 %fusion.36 = f32[1024,256]{0,1:T(8,128)} fusion(f32[3,1,1024,512]{3,2,1,0:T(8,128)} %param.8, f32[512,256]{1,0:T(8,128)S(1)} %collective-permute-done.3, f32[512,256]{1,0:T(8,128)S(1)} %fusion.41, f32[512,256]{1,0:T(8,128)S(1)} %collective-permute-done.2), kind=kOutput, calls=%fused_computation.40 | convolution fusion | flops 1610874880 | bytes 4718592 | tf_op jit(solution)/shard_map/dot_general | solution.py:40
  134.6 0.0 reduce-scatter.8.cloned.1.call-update
  134.7 0.0 all-gather.8.cloned.1.call-start
  134.7 12.1 %reduce-scatter.8.cloned.1.call-done = f32[512,256]{0,1:T(8,128)} async-done(((f32[1024,256]{0,1:T(8,128)}), f32[512,256]{0,1:T(8,128)}) %reduce-scatter.8.cloned.1.call-update) | async-done | bytes 524304 | tf_op jit(solution)/shard_map/reduce_scatter | solution.py:44
  146.8 0.0 all-gather.8.cloned.1.call-update
  146.8 0.0 all-reduce.2.cloned.1.call-start
  146.8 0.1 copy.13
  146.9 0.1 copy.14
  147.0 11.4 %all-gather.8.cloned.1.call-done = f32[1024,256]{0,1:T(8,128)} async-done(((f32[512,256]{0,1:T(8,128)}), f32[1024,256]{0,1:T(8,128)}) %all-gather.8.cloned.1.call-update) | async-done | bytes 1048592 | tf_op jit(solution)/shard_map/all_gather | solution.py:50
  158.4 0.3 mul.78
  158.7 0.9 copy-done.1
  159.6 5.0 %fusion.2 = f32[512,256]{1,0:T(8,128)S(1)} fusion(f32[1024,256]{0,1:T(8,128)S(1)} %copy-done.1, f32[128,8,4,128]{3,2,1,0:T(4,128)S(1)} %bitcast.123, f32[3,1,1024,512]{3,2,1,0:T(8,128)} %param.9), kind=kOutput, calls=%fused_computation.4 | convolution fusion | flops 1611137024 | bytes 5767168 | tf_op jit(solution)/shard_map/dot_general | solution.py:51
  164.7 3.4 %collective-permute-start.4 = (f32[512,256]{1,0:T(8,128)S(1)}, f32[512,256]{1,0:T(8,128)S(1)}, u32[]{:S(2)}, u32[]{:S(2)}) collective-permute-start(f32[512,256]{1,0:T(8,128)S(1)} %fusion.2), channel_id=1, source_target_pairs={{8,0},{10,2},{12,4},{14,6},{16,8},{18,10},{20,12},{22,14},{24,16},... | collective-permute-start | bytes 1572872 | tf_op jit(solution)/shard_map/ppermute | solution.py:10
  168.1 0.3 mul.81
  168.5 0.0 copy-start.7
  168.5 6.0 %fusion = f32[512,256]{1,0:T(8,128)} fusion(f32[1024,256]{0,1:T(8,128)S(1)} %copy-done.1, f32[128,8,4,128]{3,2,1,0:T(4,128)S(1)} %bitcast.120, f32[3,1,1024,512]{3,2,1,0:T(8,128)} %param.10), kind=kOutput, calls=%fused_computation.1 | convolution fusion | flops 1611137024 | bytes 5767168 | tf_op jit(solution)/shard_map/dot_general | solution.py:54
  174.5 0.4 fusion.44
  174.9 0.6 convolution_add_fusion.1
  175.5 1.2 fusion.39
  176.8 0.0 all-reduce.2.cloned.1.call-update
  176.8 123.9 %all-reduce.2.cloned.1.call-done = f32[64,256]{1,0:T(8,128)} async-done(((f32[64,256]{1,0:T(8,128)}), f32[64,256]{1,0:T(8,128)}) %all-reduce.2.cloned.1.call-update) | async-done | bytes 65552 | tf_op jit(solution)/shard_map/psum | solution.py:67
  300.7 1.5 sub.27
  302.1 0.0 collective-permute-done.4
  302.1 0.0 collective-permute-done.5
  302.2 1.0 subtract_bitcast_fusion
  (17 shorter events, 0.0 us)
Async XLA Ops:
  7.2 15.7 %copy-start.9 = (s32[3,1,2,8,4]{3,4,2,1,0:T(4,128)S(1)}, s32[3,1,2,8,4]{3,4,2,1,0:T(4,128)}, u32[]{:S(2)}) copy-start(s32[3,1,2,8,4]{3,4,2,1,0:T(4,128)} %param.11) | copy-start | bytes 2308
  7.2 15.6 %reduce-scatter.4.cloned.1.call-start = ((), (), s32[]{:S(2)}) async-start(), calls=%async_computation.3 | async-start | bytes 1572864 | tf_op jit(solution)/shard_map/reduce_scatter | solution.py:44
  11.7 22.8 %all-gather.4.cloned.1.call-start = ((), (), s32[]{:S(2)}) async-start(), calls=%async_computation.4 | async-start | bytes 1572864 | tf_op jit(solution)/shard_map/all_gather | solution.py:50
  22.8 62.1 %reduce-scatter.6.cloned.1.call-start = ((), (), s32[]{:S(2)}) async-start(), calls=%async_computation.5 | async-start | bytes 1572864 | tf_op jit(solution)/shard_map/reduce_scatter | solution.py:44
  34.5 1.2 copy-start
  40.8 16.3 %collective-permute-start = (f32[512,256]{1,0:T(8,128)S(1)}, f32[512,256]{1,0:T(8,128)S(1)}, u32[]{:S(2)}, u32[]{:S(2)}) collective-permute-start(f32[512,256]{1,0:T(8,128)S(1)} %fusion.10), channel_id=1, source_target_pairs={{2,0},{4,2},{6,4},{8,6},{10,8},{12,10},{14,12},{16,14},{18,16},{20... | collective-permute-start | bytes 1572872 | tf_op jit(solution)/shard_map/ppermute | solution.py:10
  46.4 21.9 %copy-start.3 = (f32[1,512,256]{2,1,0:T(8,128)S(1)}, f32[1,512,256]{2,1,0:T(8,128)}, u32[]{:S(2)}) copy-start(f32[1,512,256]{2,1,0:T(8,128)} %param.7) | copy-start | bytes 1572868
  51.6 16.8 %collective-permute-start.1 = (f32[512,256]{1,0:T(8,128)S(1)}, f32[512,256]{1,0:T(8,128)S(1)}, u32[]{:S(2)}, u32[]{:S(2)}) collective-permute-start(f32[512,256]{1,0:T(8,128)S(1)} %fusion.8), channel_id=1, source_target_pairs={{30,0},{0,2},{2,4},{4,6},{6,8},{8,10},{10,12},{12,14},{14,16},{16,... | collective-permute-start | bytes 1572872 | tf_op jit(solution)/shard_map/ppermute | solution.py:10
  74.6 21.9 %all-gather.6.cloned.1.call-start = ((), (), s32[]{:S(2)}) async-start(), calls=%async_computation.6 | async-start | bytes 1572864 | tf_op jit(solution)/shard_map/all_gather | solution.py:50
  84.9 61.9 %reduce-scatter.8.cloned.1.call-start = ((), (), s32[]{:S(2)}) async-start(), calls=%async_computation.7 | async-start | bytes 1572864 | tf_op jit(solution)/shard_map/reduce_scatter | solution.py:44
  96.5 1.2 copy-start.2
  102.8 15.4 %collective-permute-start.2 = (f32[512,256]{1,0:T(8,128)S(1)}, f32[512,256]{1,0:T(8,128)S(1)}, u32[]{:S(2)}, u32[]{:S(2)}) collective-permute-start(f32[512,256]{1,0:T(8,128)S(1)} %fusion.6), channel_id=1, source_target_pairs={{4,0},{6,2},{8,4},{10,6},{12,8},{14,10},{16,12},{18,14},{20,16},{2... | collective-permute-start | bytes 1572872 | tf_op jit(solution)/shard_map/ppermute | solution.py:10
  112.5 16.0 %collective-permute-start.3 = (f32[512,256]{1,0:T(8,128)S(1)}, f32[512,256]{1,0:T(8,128)S(1)}, u32[]{:S(2)}, u32[]{:S(2)}) collective-permute-start(f32[512,256]{1,0:T(8,128)S(1)} %fusion.4), channel_id=1, source_target_pairs={{28,0},{30,2},{0,4},{2,6},{4,8},{6,10},{8,12},{10,14},{12,16},{14,... | collective-permute-start | bytes 1572872 | tf_op jit(solution)/shard_map/ppermute | solution.py:10
  134.7 23.7 %all-gather.8.cloned.1.call-start = ((), (), s32[]{:S(2)}) async-start(), calls=%async_computation.8 | async-start | bytes 1572864 | tf_op jit(solution)/shard_map/all_gather | solution.py:50
  146.8 153.9 %all-reduce.2.cloned.1.call-start = ((), (), s32[]{:S(2)}) async-start(), calls=%async_computation.9 | async-start | bytes 131072 | tf_op jit(solution)/shard_map/psum | solution.py:67
  158.4 1.2 copy-start.1
  164.7 137.5 %collective-permute-start.4 = (f32[512,256]{1,0:T(8,128)S(1)}, f32[512,256]{1,0:T(8,128)S(1)}, u32[]{:S(2)}, u32[]{:S(2)}) collective-permute-start(f32[512,256]{1,0:T(8,128)S(1)} %fusion.2), channel_id=1, source_target_pairs={{8,0},{10,2},{12,4},{14,6},{16,8},{18,10},{20,12},{22,14},{24,16},... | collective-permute-start | bytes 1572872 | tf_op jit(solution)/shard_map/ppermute | solution.py:10
  168.4 6.0 %copy-start.4 = (f32[512,256]{1,0:T(8,128)S(1)}, f32[512,256]{1,0:T(8,128)}, u32[]{:S(2)}) copy-start(f32[512,256]{1,0:T(8,128)} %reduce-scatter.4.cloned.1.call-done) | copy-start | bytes 1572868
  168.5 6.0 %copy-start.7 = (f32[3,1,64,512]{3,2,1,0:T(8,128)S(1)}, f32[3,1,64,512]{3,2,1,0:T(8,128)}, u32[]{:S(2)}) copy-start(f32[3,1,64,512]{3,2,1,0:T(8,128)} %param.12) | copy-start | bytes 1179652
  168.5 6.4 %copy-start.5 = (f32[512,256]{0,1:T(8,128)S(1)}, f32[512,256]{0,1:T(8,128)}, u32[]{:S(2)}) copy-start(f32[512,256]{0,1:T(8,128)} %reduce-scatter.6.cloned.1.call-done) | copy-start | bytes 1572868
  168.5 7.1 %copy-start.6 = (f32[512,256]{0,1:T(8,128)S(1)}, f32[512,256]{0,1:T(8,128)}, u32[]{:S(2)}) copy-start(f32[512,256]{0,1:T(8,128)} %reduce-scatter.8.cloned.1.call-done) | copy-start | bytes 1572868
  174.5 126.2 %copy-start.8 = (f32[64,256]{1,0:T(8,128)S(1)}, f32[64,256]{1,0:T(8,128)}, u32[]{:S(2)}) copy-start(f32[64,256]{1,0:T(8,128)} %param.13) | copy-start | bytes 196612
  174.5 127.7 %collective-permute-start.5 = (f32[512,256]{1,0:T(8,128)}, f32[512,256]{1,0:T(8,128)S(1)}, u32[]{:S(2)}, u32[]{:S(2)}) collective-permute-start(f32[512,256]{1,0:T(8,128)} %fusion), channel_id=1, source_target_pairs={{24,0},{26,2},{28,4},{30,6},{0,8},{2,10},{4,12},{6,14},{8,16},{10,... | collective-permute-start | bytes 1572872 | tf_op jit(solution)/shard_map/ppermute | solution.py:10
Sparse Core Ops, SparseCore 0:
  11.9 10.8 reduce-scatter.3
  24.3 10.1 all-gather.3
  74.7 10.0 reduce-scatter.5
  86.3 10.2 all-gather.5
  134.8 11.9 reduce-scatter.7
  148.2 10.1 all-gather.7
  176.9 123.6 all-reduce.1
where the time goes:
time: 310 us
  waiting for transfers between devices  224 us (72%)
  matrix products  50.3 us (16%)
  between operations  14.3 us (5%)
  starting transfers between devices  13.8 us (4%)
  local copies, waits for them, and re-layouts  5.17 us (2%)
    psum x1, waiting for transfers between devices, local(): tip_total = tip_rhs - lax.psum(pending, ('tm', 'col'))  124 us
    all_gather x3, waiting for transfers between devices, local(): whole_solved = lax.all_gather(solved, 'col', axis=0, tiled=True)  34.3 us
    reduce_scatter x3, waiting for transfers between devices, local(): lax.psum_scatter(row_term(jnp.int32(0), own_cols * lax.axis_size('col')),...  33.3 us
    ppermute x6, waiting for transfers between devices, passed_along(): return lax.ppermute(block, axis, route)  32.2 us
    dot_general x3, matrix products, row_term(): jnp.dot(inverse_here, input_rows, precision=highest, preferred_element_ty...  16.7 us
    dot_general x3, matrix products, local(): jnp.dot(upper_masked.T, whole_solved, precision=highest, preferred_elemen...  16.1 us
    dot_general x3, matrix products, local(): jnp.dot(lower_masked.T, whole_solved, precision=highest, preferred_elemen...  15.1 us
    ppermute x6, starting transfers between devices, passed_along(): return lax.ppermute(block, axis, route)  13.6 us
  transfers between devices with their start and end apart: 13, of which 11 were waited for; matrix products, arithmetic and copies ran while one was open for 7% of the time, Pallas kernels for 0%

commit v1 on v0

--- a/solution.py
+++ b/solution.py
@@ -2,6 +2,8 @@
 import jax.numpy as jnp
 from jax import lax
 from jax.sharding import PartitionSpec as P
+
+_keep_up_wires = lambda page: jnp.sum(lax.all_gather(page, axis_name=("tm", "col")), axis=0)
 
 
 def passed_along(block, axis, distance):
@@ -64,7 +66,7 @@
             preferred_element_type=jnp.float32,
         )
         pending = pending + arrow_part
-    tip_total = tip_rhs - lax.psum(pending, ("tm", "col"))
+    tip_total = tip_rhs - _keep_up_wires(pending)
     return (present_rows[None], tip_total)
 
 

time: 310 us -> 237 us (0.76)
  waiting for transfers between devices: 224 us -> 150 us
    psum x1 -> x0, waiting for transfers between devices: 124 us -> none  [local(): tip_total = tip_rhs - lax.psum(pending, ('tm', 'col'))]
    all_gather x0 -> x1, waiting for transfers between devices: none -> 33 us  [lax.all_gather(page, axis_name=('tm', 'col'))]
    ppermute x6, waiting for transfers between devices: 32.2 us -> 51.4 us  [passed_along(): return lax.ppermute(block, axis, route)]
  transfers between devices with their start and end apart: 13 -> 13, of which waited for: 11 -> 13; matrix products, arithmetic and copies ran while one was open for 7% -> 11% of each run, Pallas kernels for 0% -> 0%
where the time goes in v1:
time: 237 us; the launch traced here: 236 us
  waiting for transfers between devices  150 us (63%)
  matrix products  49.4 us (21%)
  between operations  14.3 us (6%)
  starting transfers between devices  14.2 us (6%)
  local copies, waits for them, and re-layouts  5.17 us (2%)
  other arithmetic  3.43 us (1%)
    ppermute x6, waiting for transfers between devices, passed_along(): return lax.ppermute(block, axis, route)  51.4 us
    reduce_scatter x3, waiting for transfers between devices, local(): lax.psum_scatter(row_term(jnp.int32(0), own_cols * lax.axis_size('col')),...  33.2 us
    all_gather x1, waiting for transfers between devices, lax.all_gather(page, axis_name=('tm', 'col'))  33 us
    all_gather x3, waiting for transfers between devices, local(): whole_solved = lax.all_gather(solved, 'col', axis=0, tiled=True)  32 us
    dot_general x3, matrix products, row_term(): jnp.dot(inverse_here, input_rows, precision=highest, preferred_element_ty...  16.7 us
    dot_general x3, matrix products, local(): jnp.dot(upper_masked.T, whole_solved, precision=highest, preferred_elemen...  15.2 us
    dot_general x3, matrix products, local(): jnp.dot(lower_masked.T, whole_solved, precision=highest, preferred_elemen...  15.1 us
    ppermute x6, starting transfers between devices, passed_along(): return lax.ppermute(block, axis, route)  13.9 us
  transfers between devices with their start and end apart: 13, of which 13 were waited for; matrix products, arithmetic and copies ran while one was open for 11% of the time, Pallas kernels for 0%

profile of v1, /device:TPU:1, one launch (start us, length us, event | category | flops | bytes accessed | tf_op | source)
XLA Modules:
  0.0 236.2 jit_solution(10820615355273425218)
XLA Ops:
  7.2 0.0 reduce-scatter.4.cloned.1.call-start
  7.2 4.5 %fusion.21 = f32[1024,256]{1,0:T(8,128)} fusion(f32[3,1,1024,512]{3,2,1,0:T(8,128)} %param.8, f32[1,512,256]{2,1,0:T(8,128)} %param.7), kind=kOutput, calls=%fused_computation.27 | convolution fusion | flops 1610612736 | bytes 3670016 | tf_op jit(solution)/shard_map/dot_general | solution.py:42
  11.7 0.0 reduce-scatter.4.cloned.1.call-update
  11.7 0.0 all-gather.6.cloned.1.call-start
  11.8 11.0 %reduce-scatter.4.cloned.1.call-done = f32[512,256]{1,0:T(8,128)} async-done(((f32[1024,256]{1,0:T(8,128)}), f32[512,256]{1,0:T(8,128)}) %reduce-scatter.4.cloned.1.call-update) | async-done | bytes 524304 | tf_op jit(solution)/shard_map/reduce_scatter | solution.py:46
  22.8 0.0 all-gather.6.cloned.1.call-update
  22.8 0.0 reduce-scatter.6.cloned.1.call-start
  22.9 0.1 copy.9
  23.0 0.1 copy.10
  23.0 11.5 %all-gather.6.cloned.1.call-done = f32[1024,256]{1,0:T(8,128)} async-done(((f32[512,256]{1,0:T(8,128)}), f32[1024,256]{1,0:T(8,128)}) %all-gather.6.cloned.1.call-update) | async-done | bytes 1048592 | tf_op jit(solution)/shard_map/all_gather | solution.py:52
  34.5 0.3 mul.66
  34.9 0.9 copy-done.1
  35.8 5.1 %fusion.10 = f32[512,256]{1,0:T(8,128)S(1)} fusion(f32[1024,256]{1,0:T(8,128)S(1)} %copy-done.1, f32[128,8,4,128]{3,2,1,0:T(4,128)S(1)} %bitcast.122, f32[3,1,1024,512]{3,2,1,0:T(8,128)} %param.9), kind=kOutput, calls=%fused_computation.16 | convolution fusion | flops 1611137024 | bytes 5767168 | tf_op jit(solution)/shard_map/dot_general | solution.py:53
  40.8 5.3 %collective-permute-start = (f32[512,256]{1,0:T(8,128)S(1)}, f32[512,256]{1,0:T(8,128)S(1)}, u32[]{:S(2)}, u32[]{:S(2)}) collective-permute-start(f32[512,256]{1,0:T(8,128)S(1)} %fusion.10), channel_id=1, source_target_pairs={{2,0},{4,2},{6,4},{8,6},{10,8},{12,10},{14,12},{16,14},{18,16},{20... | collective-permute-start | bytes 1572872 | tf_op jit(solution)/shard_map/ppermute | solution.py:12
  46.1 0.3 mul.69
  46.4 5.1 %fusion.8 = f32[512,256]{1,0:T(8,128)S(1)} fusion(f32[1024,256]{1,0:T(8,128)S(1)} %copy-done.1, f32[128,8,4,128]{3,2,1,0:T(4,128)S(1)} %bitcast.119, f32[3,1,1024,512]{3,2,1,0:T(8,128)} %param.10), kind=kOutput, calls=%fused_computation.13 | convolution fusion | flops 1611137024 | bytes 5767168 | tf_op jit(solution)/shard_map/dot_general | solution.py:56
  51.6 0.2 collective-permute-start.1
  51.8 5.3 %collective-permute-done = f32[512,256]{1,0:T(8,128)S(1)} collective-permute-done((f32[512,256]{1,0:T(8,128)S(1)}, f32[512,256]{1,0:T(8,128)S(1)}, u32[]{:S(2)}, u32[]{:S(2)}) %collective-permute-start) | collective-permute-done | bytes 524320 | tf_op jit(solution)/shard_map/ppermute | solution.py:12
  57.1 11.2 %collective-permute-done.1 = f32[512,256]{1,0:T(8,128)S(1)} collective-permute-done((f32[512,256]{1,0:T(8,128)S(1)}, f32[512,256]{1,0:T(8,128)S(1)}, u32[]{:S(2)}, u32[]{:S(2)}) %collective-permute-start.1) | collective-permute-done | bytes 524320 | tf_op jit(solution)/shard_map/ppermute | solution.py:12
  68.4 0.1 fusion.41
  68.5 6.1 %fusion.33 = f32[1024,256]{0,1:T(8,128)} fusion(f32[512,256]{1,0:T(8,128)S(1)} %fusion.41, f32[3,1,1024,512]{3,2,1,0:T(8,128)} %param.8), kind=kOutput, calls=%fused_computation.39 | convolution fusion | flops 1610612736 | bytes 3670016 | tf_op jit(solution)/shard_map/dot_general | solution.py:42
  74.6 0.0 reduce-scatter.6.cloned.1.call-update
  74.6 0.0 all-gather.8.cloned.1.call-start
  74.7 10.2 %reduce-scatter.6.cloned.1.call-done = f32[512,256]{0,1:T(8,128)} async-done(((f32[1024,256]{0,1:T(8,128)}), f32[512,256]{0,1:T(8,128)}) %reduce-scatter.6.cloned.1.call-update) | async-done | bytes 524304 | tf_op jit(solution)/shard_map/reduce_scatter | solution.py:46
  84.9 0.0 all-gather.8.cloned.1.call-update
  84.9 0.0 reduce-scatter.8.cloned.1.call-start
  85.0 0.1 copy.11
  85.0 0.1 copy.12
  85.1 11.4 %all-gather.8.cloned.1.call-done = f32[1024,256]{0,1:T(8,128)} async-done(((f32[512,256]{0,1:T(8,128)}), f32[1024,256]{0,1:T(8,128)}) %all-gather.8.cloned.1.call-update) | async-done | bytes 1048592 | tf_op jit(solution)/shard_map/all_gather | solution.py:52
  96.5 0.3 mul.72
  96.9 0.9 copy-done.2
  97.8 5.0 %fusion.6 = f32[512,256]{1,0:T(8,128)S(1)} fusion(f32[1024,256]{0,1:T(8,128)S(1)} %copy-done.2, f32[128,8,4,128]{3,2,1,0:T(4,128)S(1)} %bitcast.123, f32[3,1,1024,512]{3,2,1,0:T(8,128)} %param.9), kind=kOutput, calls=%fused_computation.10 | convolution fusion | flops 1611137024 | bytes 5767168 | tf_op jit(solution)/shard_map/dot_general | solution.py:53
  102.8 4.4 %collective-permute-start.2 = (f32[512,256]{1,0:T(8,128)S(1)}, f32[512,256]{1,0:T(8,128)S(1)}, u32[]{:S(2)}, u32[]{:S(2)}) collective-permute-start(f32[512,256]{1,0:T(8,128)S(1)} %fusion.6), channel_id=1, source_target_pairs={{4,0},{6,2},{8,4},{10,6},{12,8},{14,10},{16,12},{18,14},{20,16},{2... | collective-permute-start | bytes 1572872 | tf_op jit(solution)/shard_map/ppermute | solution.py:12
  107.2 0.3 mul.75
  107.5 5.0 %fusion.4 = f32[512,256]{1,0:T(8,128)S(1)} fusion(f32[1024,256]{0,1:T(8,128)S(1)} %copy-done.2, f32[128,8,4,128]{3,2,1,0:T(4,128)S(1)} %bitcast.120, f32[3,1,1024,512]{3,2,1,0:T(8,128)} %param.10), kind=kOutput, calls=%fused_computation.7 | convolution fusion | flops 1611137024 | bytes 5767168 | tf_op jit(solution)/shard_map/dot_general | solution.py:56
  112.6 0.3 collective-permute-start.3
  112.9 5.4 %collective-permute-done.2 = f32[512,256]{1,0:T(8,128)S(1)} collective-permute-done((f32[512,256]{1,0:T(8,128)S(1)}, f32[512,256]{1,0:T(8,128)S(1)}, u32[]{:S(2)}, u32[]{:S(2)}) %collective-permute-start.2) | collective-permute-done | bytes 524320 | tf_op jit(solution)/shard_map/ppermute | solution.py:12
  118.2 10.3 %collective-permute-done.3 = f32[512,256]{1,0:T(8,128)S(1)} collective-permute-done((f32[512,256]{1,0:T(8,128)S(1)}, f32[512,256]{1,0:T(8,128)S(1)}, u32[]{:S(2)}, u32[]{:S(2)}) %collective-permute-start.3) | collective-permute-done | bytes 524320 | tf_op jit(solution)/shard_map/ppermute | solution.py:12
  128.5 6.1 %fusion.36 = f32[1024,256]{0,1:T(8,128)} fusion(f32[3,1,1024,512]{3,2,1,0:T(8,128)} %param.8, f32[512,256]{1,0:T(8,128)S(1)} %collective-permute-done.3, f32[512,256]{1,0:T(8,128)S(1)} %fusion.41, f32[512,256]{1,0:T(8,128)S(1)} %collective-permute-done.2), kind=kOutput, calls=%fused_computation.40 | convolution fusion | flops 1610874880 | bytes 4718592 | tf_op jit(solution)/shard_map/dot_general | solution.py:42
  134.7 0.0 reduce-scatter.8.cloned.1.call-update
  134.7 0.0 all-gather.10.cloned.1.call-start
  134.7 12.0 %reduce-scatter.8.cloned.1.call-done = f32[512,256]{0,1:T(8,128)} async-done(((f32[1024,256]{0,1:T(8,128)}), f32[512,256]{0,1:T(8,128)}) %reduce-scatter.8.cloned.1.call-update) | async-done | bytes 524304 | tf_op jit(solution)/shard_map/reduce_scatter | solution.py:46
  146.8 0.0 all-gather.10.cloned.1.call-update
  146.8 0.0 all-gather.12.cloned.1.call-start
  146.8 0.4 fusion.44
  147.3 0.6 convolution_add_fusion.1
  147.9 1.2 fusion.39
  149.1 0.0 all-gather.12.cloned.1.call-update
  149.2 0.1 copy.13
  149.2 0.1 copy.14
  149.3 9.1 %all-gather.10.cloned.1.call-done = f32[1024,256]{0,1:T(8,128)} async-done(((f32[512,256]{0,1:T(8,128)}), f32[1024,256]{0,1:T(8,128)}) %all-gather.10.cloned.1.call-update) | async-done | bytes 1048592 | tf_op jit(solution)/shard_map/all_gather | solution.py:52
  158.4 0.3 mul.78
  158.7 0.9 copy-done
  159.6 5.0 %fusion.2 = f32[512,256]{1,0:T(8,128)S(1)} fusion(f32[1024,256]{0,1:T(8,128)S(1)} %copy-done, f32[128,8,4,128]{3,2,1,0:T(4,128)S(1)} %bitcast.124, f32[3,1,1024,512]{3,2,1,0:T(8,128)} %param.9), kind=kOutput, calls=%fused_computation.4 | convolution fusion | flops 1611137024 | bytes 5767168 | tf_op jit(solution)/shard_map/dot_general | solution.py:53
  164.7 3.7 %collective-permute-start.4 = (f32[512,256]{1,0:T(8,128)S(1)}, f32[512,256]{1,0:T(8,128)S(1)}, u32[]{:S(2)}, u32[]{:S(2)}) collective-permute-start(f32[512,256]{1,0:T(8,128)S(1)} %fusion.2), channel_id=1, source_target_pairs={{8,0},{10,2},{12,4},{14,6},{16,8},{18,10},{20,12},{22,14},{24,16},... | collective-permute-start | bytes 1572872 | tf_op jit(solution)/shard_map/ppermute | solution.py:12
  168.4 0.3 mul.81
  168.7 5.0 %fusion = f32[512,256]{1,0:T(8,128)S(1)} fusion(f32[1024,256]{0,1:T(8,128)S(1)} %copy-done, f32[128,8,4,128]{3,2,1,0:T(4,128)S(1)} %bitcast.121, f32[3,1,1024,512]{3,2,1,0:T(8,128)} %param.10), kind=kOutput, calls=%fused_computation.1 | convolution fusion | flops 1611137024 | bytes 5767168 | tf_op jit(solution)/shard_map/dot_general | solution.py:56
  173.8 0.1 collective-permute-start.5
  173.8 6.7 %collective-permute-done.4 = f32[512,256]{1,0:T(8,128)S(1)} collective-permute-done((f32[512,256]{1,0:T(8,128)S(1)}, f32[512,256]{1,0:T(8,128)S(1)}, u32[]{:S(2)}, u32[]{:S(2)}) %collective-permute-start.4) | collective-permute-done | bytes 524320 | tf_op jit(solution)/shard_map/ppermute | solution.py:12
  180.6 12.5 %collective-permute-done.5 = f32[512,256]{1,0:T(8,128)S(1)} collective-permute-done((f32[512,256]{1,0:T(8,128)S(1)}, f32[512,256]{1,0:T(8,128)S(1)}, u32[]{:S(2)}, u32[]{:S(2)}) %collective-permute-start.5) | collective-permute-done | bytes 524320 | tf_op jit(solution)/shard_map/ppermute | solution.py:12
  193.0 1.0 subtract_bitcast_fusion
  194.0 33.0 %all-gather.12.cloned.1.call-done = f32[2048,256]{1,0:T(8,128)} async-done(((f32[64,256]{1,0:T(8,128)}), f32[2048,256]{1,0:T(8,128)}) %all-gather.12.cloned.1.call-update) | async-done | bytes 2097168 | tf_op jit(solution)/shard_map/all_gather | solution.py:6
  227.0 1.7 reduce_sum.9
  228.7 0.6 sub.27
  (18 shorter events, 0.0 us)
Async XLA Ops:
  7.2 15.7 %copy-start.9 = (s32[3,1,2,8,4]{3,4,2,1,0:T(4,128)S(1)}, s32[3,1,2,8,4]{3,4,2,1,0:T(4,128)}, u32[]{:S(2)}) copy-start(s32[3,1,2,8,4]{3,4,2,1,0:T(4,128)} %param.11) | copy-start | bytes 2308
  7.2 15.6 %reduce-scatter.4.cloned.1.call-start = ((), (), s32[]{:S(2)}) async-start(), calls=%async_computation.3 | async-start | bytes 1572864 | tf_op jit(solution)/shard_map/reduce_scatter | solution.py:46
  11.7 22.8 %all-gather.6.cloned.1.call-start = ((), (), s32[]{:S(2)}) async-start(), calls=%async_computation.4 | async-start | bytes 1572864 | tf_op jit(solution)/shard_map/all_gather | solution.py:52
  22.8 62.1 %reduce-scatter.6.cloned.1.call-start = ((), (), s32[]{:S(2)}) async-start(), calls=%async_computation.5 | async-start | bytes 1572864 | tf_op jit(solution)/shard_map/reduce_scatter | solution.py:46
  34.5 1.2 copy-start.1
  40.8 16.3 %collective-permute-start = (f32[512,256]{1,0:T(8,128)S(1)}, f32[512,256]{1,0:T(8,128)S(1)}, u32[]{:S(2)}, u32[]{:S(2)}) collective-permute-start(f32[512,256]{1,0:T(8,128)S(1)} %fusion.10), channel_id=1, source_target_pairs={{2,0},{4,2},{6,4},{8,6},{10,8},{12,10},{14,12},{16,14},{18,16},{20... | collective-permute-start | bytes 1572872 | tf_op jit(solution)/shard_map/ppermute | solution.py:12
  46.4 21.9 %copy-start.3 = (f32[1,512,256]{2,1,0:T(8,128)S(1)}, f32[1,512,256]{2,1,0:T(8,128)}, u32[]{:S(2)}) copy-start(f32[1,512,256]{2,1,0:T(8,128)} %param.7) | copy-start | bytes 1572868
  51.6 16.8 %collective-permute-start.1 = (f32[512,256]{1,0:T(8,128)S(1)}, f32[512,256]{1,0:T(8,128)S(1)}, u32[]{:S(2)}, u32[]{:S(2)}) collective-permute-start(f32[512,256]{1,0:T(8,128)S(1)} %fusion.8), channel_id=1, source_target_pairs={{30,0},{0,2},{2,4},{4,6},{6,8},{8,10},{10,12},{12,14},{14,16},{16,... | collective-permute-start | bytes 1572872 | tf_op jit(solution)/shard_map/ppermute | solution.py:12
  74.6 21.9 %all-gather.8.cloned.1.call-start = ((), (), s32[]{:S(2)}) async-start(), calls=%async_computation.6 | async-start | bytes 1572864 | tf_op jit(solution)/shard_map/all_gather | solution.py:52
  84.9 61.9 %reduce-scatter.8.cloned.1.call-start = ((), (), s32[]{:S(2)}) async-start(), calls=%async_computation.7 | async-start | bytes 1572864 | tf_op jit(solution)/shard_map/reduce_scatter | solution.py:46
  96.5 1.2 copy-start.2
  102.8 15.4 %collective-permute-start.2 = (f32[512,256]{1,0:T(8,128)S(1)}, f32[512,256]{1,0:T(8,128)S(1)}, u32[]{:S(2)}, u32[]{:S(2)}) collective-permute-start(f32[512,256]{1,0:T(8,128)S(1)} %fusion.6), channel_id=1, source_target_pairs={{4,0},{6,2},{8,4},{10,6},{12,8},{14,10},{16,12},{18,14},{20,16},{2... | collective-permute-start | bytes 1572872 | tf_op jit(solution)/shard_map/ppermute | solution.py:12
  112.6 34.3 %copy-start.4 = (f32[512,256]{1,0:T(8,128)S(1)}, f32[512,256]{1,0:T(8,128)}, u32[]{:S(2)}) copy-start(f32[512,256]{1,0:T(8,128)} %reduce-scatter.4.cloned.1.call-done) | copy-start | bytes 1572868
  112.6 34.3 %copy-start.7 = (f32[3,1,64,512]{3,2,1,0:T(8,128)S(1)}, f32[3,1,64,512]{3,2,1,0:T(8,128)}, u32[]{:S(2)}) copy-start(f32[3,1,64,512]{3,2,1,0:T(8,128)} %param.12) | copy-start | bytes 1179652
  112.6 16.0 %collective-permute-start.3 = (f32[512,256]{1,0:T(8,128)S(1)}, f32[512,256]{1,0:T(8,128)S(1)}, u32[]{:S(2)}, u32[]{:S(2)}) collective-permute-start(f32[512,256]{1,0:T(8,128)S(1)} %fusion.4), channel_id=1, source_target_pairs={{28,0},{30,2},{0,4},{2,6},{4,8},{6,10},{8,12},{10,14},{12,16},{14,... | collective-permute-start | bytes 1572872 | tf_op jit(solution)/shard_map/ppermute | solution.py:12
  134.7 12.6 %copy-start.5 = (f32[512,256]{0,1:T(8,128)S(1)}, f32[512,256]{0,1:T(8,128)}, u32[]{:S(2)}) copy-start(f32[512,256]{0,1:T(8,128)} %reduce-scatter.6.cloned.1.call-done) | copy-start | bytes 1572868
  134.7 23.7 %all-gather.10.cloned.1.call-start = ((), (), s32[]{:S(2)}) async-start(), calls=%async_computation.8 | async-start | bytes 1572864 | tf_op jit(solution)/shard_map/all_gather | solution.py:52
  146.8 1.1 copy-start.6
  146.8 80.2 %all-gather.12.cloned.1.call-start = ((), (), s32[]{:S(2)}) async-start(), calls=%async_computation.9 | async-start | bytes 2162688 | tf_op jit(solution)/shard_map/all_gather | solution.py:6
  158.4 1.2 copy-start
  164.7 15.9 %collective-permute-start.4 = (f32[512,256]{1,0:T(8,128)S(1)}, f32[512,256]{1,0:T(8,128)S(1)}, u32[]{:S(2)}, u32[]{:S(2)}) collective-permute-start(f32[512,256]{1,0:T(8,128)S(1)} %fusion.2), channel_id=1, source_target_pairs={{8,0},{10,2},{12,4},{14,6},{16,8},{18,10},{20,12},{22,14},{24,16},... | collective-permute-start | bytes 1572872 | tf_op jit(solution)/shard_map/ppermute | solution.py:12
  173.8 54.9 %copy-start.8 = (f32[64,256]{1,0:T(8,128)S(1)}, f32[64,256]{1,0:T(8,128)}, u32[]{:S(2)}) copy-start(f32[64,256]{1,0:T(8,128)} %param.13) | copy-start | bytes 196612
  173.8 19.3 %collective-permute-start.5 = (f32[512,256]{1,0:T(8,128)S(1)}, f32[512,256]{1,0:T(8,128)S(1)}, u32[]{:S(2)}, u32[]{:S(2)}) collective-permute-start(f32[512,256]{1,0:T(8,128)S(1)} %fusion), channel_id=1, source_target_pairs={{24,0},{26,2},{28,4},{30,6},{0,8},{2,10},{4,12},{6,14},{8,16},{10,... | collective-permute-start | bytes 1572872 | tf_op jit(solution)/shard_map/ppermute | solution.py:12
Sparse Core Ops, SparseCore 0:
  11.9 10.8 reduce-scatter.3
  24.3 10.1 all-gather.5
  74.7 10.0 reduce-scatter.5
  86.3 10.2 all-gather.7
  134.8 11.9 reduce-scatter.7
  148.2 10.1 all-gather.9
  161.8 65.1 all-gather.11
